TPU v7x, 256 devices: a whole 4x4x8 slice. The times are simulated.
256 devices in a mesh: rows: 64 (over y_lo, z, x), blk: 4 (over y_hi, core).
Axes of the slice: x: 4, y: 4 (y_hi: 2, y_lo: 2; y = y_hi * 2 + y_lo), z: 8, core: 2. Of those that a mesh axis runs over, the one named last changes fastest.
Arguments:
- block_weight: bfloat16 [64, 4, 4, 64, 128, 128], P('rows', 'blk'), may hold values from 0.049804688 to 50
- block_row: int32 [64, 4, 4, 64], P('rows', 'blk'), may hold values from 0 to 15, as said below
- block_col: int32 [64, 4, 4, 64], P('rows', 'blk'), may hold values from 0 to 7, as said below
- block_count: int32 [64, 4, 4], P('rows', 'blk'), may hold values from 1 to 64, as said below
- block_samples: int32 [64, 4, 4, 64], P('rows', 'blk'), may hold values from 1 to 8
- row_degree: float32 [64, 4, 2048], P('rows', 'blk'), may hold values from 0.125 to 8
- col_degree: float32 [4, 1024], P('blk', 'rows'), may hold values from 1 to 8
- test_matrix: bfloat16 [4, 1024, 128], P('blk', 'rows'), may hold values from -6 to 6
Outputs:
- basis: float32 [64, 4, 2048, 128], P('rows', 'blk')
- triangle: float32 [128, 128], replicated
Inputs may be any that keep to these rules, and one draw needn't show every extreme that they name: Within one band and slab, the slots k < 64 hold distinct (block_row, block_col) pairs. `block_col`: see block_row: pairs are distinct within one band and slab. `block_count`: some band and slab has all 64 slots live in every draw.
All inputs are finite; a program needn't handle non-finite values.
Results may differ from a plain program's by a relative error of at most 0.0065.
Values may be sent and summed in bfloat16 or wider, within the bound.
A program may use at most 64 MiB of HBM per device.

v0:
```python
import jax
import jax.numpy as jnp
from jax import lax
from jax.sharding import PartitionSpec as P

scale_factor = 16.0


def passed_along(block, axis, distance):
    devices = range(lax.axis_size(axis))
    route = [((i - distance) % len(devices), i) for i in devices]
    return lax.ppermute(block, axis, route)


def tile_update(
    running, weights, rows_idx, cols_idx, live_count, samples, row_deg, slab_rows, slab_deg
):
    block_edge = weights.shape[-1]
    capacity = weights.shape[0]
    band_blocks = running.shape[0]
    slab_blocks = slab_rows.shape[0] // block_edge
    slab_tiles = slab_rows.reshape(slab_blocks, block_edge, slab_rows.shape[1])
    picked = slab_tiles[cols_idx]
    col_d = slab_deg.reshape(slab_blocks, block_edge)[cols_idx]
    row_d = row_deg.reshape(band_blocks, block_edge)[rows_idx]
    scaled_ratio = (
        scale_factor
        * weights.astype(jnp.float32)
        / (samples.astype(jnp.float32)[:, None, None] * row_d[:, :, None] * col_d[:, None, :])
    )
    entries = jnp.log(jnp.maximum(scaled_ratio, 1.0)).astype(jnp.bfloat16)
    products = jnp.einsum("kij,kjc->kic", entries, picked, preferred_element_type=jnp.float32)
    alive_mask = (jnp.arange(capacity, dtype=jnp.int32) < live_count).astype(jnp.float32)
    chooser = (rows_idx[None, :] == jnp.arange(band_blocks, dtype=jnp.int32)[:, None]).astype(
        jnp.float32
    ) * alive_mask[None, :]
    return running + jnp.einsum("rk,kic->ric", chooser, products, precision=lax.Precision.HIGHEST)


def body(
    block_weight,
    block_row,
    block_col,
    block_count,
    block_samples,
    row_degree,
    col_degree,
    test_matrix,
):
    loop_size = lax.axis_size("blk")
    position = lax.axis_index("blk")
    weights_all = block_weight[0, 0]
    rows_all = block_row[0, 0]
    cols_all = block_col[0, 0]
    counts_all = block_count[0, 0]
    samples_all = block_samples[0, 0]
    row_deg = row_degree[0, 0]
    block_edge = weights_all.shape[-1]
    band_blocks = row_deg.shape[0] // block_edge
    running = jnp.zeros((band_blocks, block_edge, test_matrix.shape[2]), jnp.float32)
    piece_pair = (test_matrix, col_degree)
    for t in range(loop_size):
        if t > 0:
            piece_pair = (
                passed_along(piece_pair[0], "blk", 1),
                passed_along(piece_pair[1].astype(jnp.bfloat16), "blk", 1).astype(jnp.float32),
            )
        slab_rows, slab_deg = (
            lax.all_gather(piece_pair[0], "rows", axis=1, tiled=True),
            lax.all_gather(piece_pair[1].astype(jnp.bfloat16), "rows", axis=1, tiled=True).astype(
                jnp.float32
            ),
        )
        slab_index = (position - t) % loop_size
        apply_slab_rows = slab_rows[0]
        apply_slab_deg = slab_deg[0]
        slab_index = jnp.asarray(slab_index)
        running = tile_update(
            running,
            lax.dynamic_index_in_dim(weights_all, slab_index, 0, keepdims=False),
            lax.dynamic_index_in_dim(rows_all, slab_index, 0, keepdims=False),
            lax.dynamic_index_in_dim(cols_all, slab_index, 0, keepdims=False),
            lax.dynamic_index_in_dim(counts_all, slab_index, 0, keepdims=False),
            lax.dynamic_index_in_dim(samples_all, slab_index, 0, keepdims=False),
            row_deg,
            apply_slab_rows,
            apply_slab_deg,
        )
    flat_rows = running.reshape(band_blocks * block_edge, running.shape[2])
    gram_local = jnp.dot(
        flat_rows.T, flat_rows, precision=lax.Precision.HIGHEST, preferred_element_type=jnp.float32
    )
    gram_total = lax.psum(gram_local, ("rows", "blk"))
    lower_factor = jnp.linalg.cholesky(gram_total)
    total_rows = flat_rows.shape[0] * lax.axis_size("rows") * loop_size
    root = jnp.sqrt(jnp.float32(total_rows))
    basis_rows = (
        lax.linalg.triangular_solve(
            lower_factor, flat_rows, left_side=False, lower=True, transpose_a=True
        )
        * root
    )
    return (basis_rows.reshape(1, 1, flat_rows.shape[0], flat_rows.shape[1]), lower_factor.T / root)


def solution(mesh):
    placed = (
        P("rows", "blk", None, None, None, None),
        P("rows", "blk", None, None),
        P("rows", "blk", None, None),
        P("rows", "blk", None),
        P("rows", "blk", None, None),
        P("rows", "blk", None),
        P("blk", "rows"),
        P("blk", "rows", None),
    )
    return jax.shard_map(
        body,
        mesh=mesh,
        in_specs=placed,
        out_specs=(P("rows", "blk", None, None), P()),
        check_vma=False,
    )
```

profile of v0, /device:TPU:1, one launch (start us, length us, event | category | flops | bytes accessed | tf_op | source)
XLA Modules:
  0.0 1118.6 jit_solution(2050559915229179514)
XLA Ops:
  7.2 4.4 collective-permute-start.1
  12.3 132.2 %all_gather.25 = bf16[1,1024,128]{2,1,0:T(8,128)(2,1)S(1)} all-gather(bf16[1,16,128]{2,1,0:T(8,128)(2,1)} %param.15), channel_id=1, replica_groups=mesh['rows'=64,'blk'=4] {'rows'}, dimensions={1}, use_global_device_ids=true | all-gather | bytes 266240 | tf_op jit(solution)/shard_map/all_gather | solution.py:69
  158.6 29.4 %collective-permute-start.2 = (bf16[1,16]{1,0:T(2,128)(2,1)S(1)}, bf16[1,16]{1,0:T(2,128)(2,1)S(1)}, u32[]{:S(2)}, u32[]{:S(2)}) collective-permute-start(bf16[1,16]{1,0:T(2,128)(2,1)S(1)} %collective-permute-done), channel_id=1, source_target_pairs={{3,0},{0,1},{1,2},{2,3},{7,4},{4,5},{5,6},{6,7},{11,8},{8,9},{9,10... | collective-permute-start | bytes 104 | tf_op jit(solution)/shard_map/ppermute | solution.py:12
  188.9 3.8 collective-permute-start.4
  193.6 127.1 %all-reduce.4 = (bf16[1024]{0:T(1024)(128)(2,1)S(1)}, bf16[1024]{0:T(1024)(128)(2,1)S(1)}, bf16[1024]{0:T(1024)(128)(2,1)S(1)}, bf16[1024]{0:T(1024)(128)(2,1)S(1)}) all-reduce(bf16[1024]{0:T(1024)(128)(2,1)S(1)} %dynamic-update-slice.4, bf16[1024]{0:T(1024)(128)(2,1)S(1)} %dynamic-update-slice.3, ...), channel_id=1, replica_groups=mesh['rows'=64,'blk'=4] {'rows'}, use_global_device_ids=true, to_apply=%add.1 | all-reduce | flops 4096 | bytes 16384
  321.4 4.1 fusion.21
  327.3 124.8 %all_gather.27 = bf16[1,1024,128]{2,1,0:T(8,128)(2,1)S(1)} all-gather(bf16[1,16,128]{2,1,0:T(8,128)(2,1)S(1)} %collective-permute-done.1), channel_id=1, replica_groups=mesh['rows'=64,'blk'=4] {'rows'}, dimensions={1}, use_global_device_ids=true | all-gather | bytes 266240 | tf_op jit(solution)/shard_map/all_gather | solution.py:69
  453.1 3.6 fusion.23
  456.7 4.4 fusion.16
  461.0 60.1 %collective-permute-start.3 = (bf16[1,16,128]{2,1,0:T(8,128)(2,1)S(1)}, bf16[1,16,128]{2,1,0:T(8,128)(2,1)S(1)}, u32[]{:S(2)}, u32[]{:S(2)}) collective-permute-start(bf16[1,16,128]{2,1,0:T(8,128)(2,1)S(1)} %collective-permute-done.1), channel_id=1, source_target_pairs={{3,0},{0,1},{1,2},{2,3},{7,4},{4,5},{5,6},{6,7},{11,8},{8,9},{9,10... | collective-permute-start | bytes 12296 | tf_op jit(solution)/shard_map/ppermute | solution.py:12
  521.1 4.4 fusion.49
  525.5 124.0 %all_gather.29 = bf16[1,1024,128]{2,1,0:T(8,128)(2,1)S(1)} all-gather(bf16[1,16,128]{2,1,0:T(8,128)(2,1)S(1)} %collective-permute-done.3), channel_id=1, replica_groups=mesh['rows'=64,'blk'=4] {'rows'}, dimensions={1}, use_global_device_ids=true | all-gather | bytes 266240 | tf_op jit(solution)/shard_map/all_gather | solution.py:69
  650.6 3.6 fusion.25
  654.2 27.5 %collective-permute-start.5 = (bf16[1,16,128]{2,1,0:T(8,128)(2,1)S(1)}, bf16[1,16,128]{2,1,0:T(8,128)(2,1)S(1)}, u32[]{:S(2)}, u32[]{:S(2)}) collective-permute-start(bf16[1,16,128]{2,1,0:T(8,128)(2,1)S(1)} %copy-done.3), channel_id=1, source_target_pairs={{3,0},{0,1},{1,2},{2,3},{7,4},{4,5},{5,6},{6,7},{11,8},{8,9},{9,10... | collective-permute-start | bytes 12296 | tf_op jit(solution)/shard_map/ppermute | solution.py:12
  681.8 4.4 fusion.52
  686.2 125.7 %all_gather.31 = bf16[1,1024,128]{2,1,0:T(8,128)(2,1)S(1)} all-gather(bf16[1,16,128]{2,1,0:T(8,128)(2,1)S(1)} %collective-permute-done.5), channel_id=1, replica_groups=mesh['rows'=64,'blk'=4] {'rows'}, dimensions={1}, use_global_device_ids=true | all-gather | bytes 266240 | tf_op jit(solution)/shard_map/all_gather | solution.py:69
  811.9 2.1 gather_fusion.11
  814.0 3.3 fusion.27
  817.4 4.4 fusion.55
  821.8 2.5 convolution_bitcast_fusion
  824.7 259.5 %all-reduce.7.cloned.1.call-done = f32[128,128]{0,1:T(8,128)} async-done(((f32[128,128]{0,1:T(8,128)}), f32[128,128]{0,1:T(8,128)}) %all-reduce.7.cloned.1.call-update) | async-done | bytes 65552 | tf_op jit(solution)/shard_map/psum | solution.py:93
  1086.0 11.7 %cholesky.16 = f32[128,128]{1,0:T(8,128)S(1)} custom-call(f32[128,128]{1,0:T(8,128)S(1)} %fusion.59), custom_call_target="Cholesky" | custom-call | tf_op jit(solution)/shard_map/jit(cholesky)/cholesky | solution.py:94
  1099.1 9.8 custom-call.6
  1109.6 1.9 fusion.20
  (77 shorter events, 24.5 us)
Async XLA Ops:
  7.2 142.5 %copy-start = (f32[1,1,2048]{2,1,0:T(1,128)S(1)}, f32[1,1,2048]{2,1,0:T(1,128)}, u32[]{:S(2)}) copy-start(f32[1,1,2048]{2,1,0:T(1,128)} %param.13) | copy-start | bytes 24580
  7.2 1077.0 %all-reduce.7.cloned.1.call-start = ((), (), s32[]{:S(2)}) async-start(), calls=%async_computation | async-start | bytes 131072 | tf_op jit(solution)/shard_map/psum | solution.py:93
  7.2 320.1 %collective-permute-start.1 = (bf16[1,16,128]{2,1,0:T(8,128)(2,1)}, bf16[1,16,128]{2,1,0:T(8,128)(2,1)S(1)}, u32[]{:S(2)}, u32[]{:S(2)}) collective-permute-start(bf16[1,16,128]{2,1,0:T(8,128)(2,1)} %param.15), channel_id=1, source_target_pairs={{3,0},{0,1},{1,2},{2,3},{7,4},{4,5},{5,6},{6,7},{11,8},{8,9},{9,10... | collective-permute-start | bytes 12296 | tf_op jit(solution)/shard_map/ppermute | solution.py:12
  12.3 146.1 %collective-permute-start = (bf16[1,16]{1,0:T(2,128)(2,1)S(1)}, bf16[1,16]{1,0:T(2,128)(2,1)S(1)}, u32[]{:S(2)}, u32[]{:S(2)}) collective-permute-start(bf16[1,16]{1,0:T(2,128)(2,1)S(1)} %get-tuple-element.33), channel_id=1, source_target_pairs={{3,0},{0,1},{1,2},{2,3},{7,4},{4,5},{5,6},{6,7},{11,8},{8,9},{9,10... | collective-permute-start | bytes 104 | tf_op jit(solution)/shard_map/ppermute | solution.py:12
  158.6 30.1 %collective-permute-start.2 = (bf16[1,16]{1,0:T(2,128)(2,1)S(1)}, bf16[1,16]{1,0:T(2,128)(2,1)S(1)}, u32[]{:S(2)}, u32[]{:S(2)}) collective-permute-start(bf16[1,16]{1,0:T(2,128)(2,1)S(1)} %collective-permute-done), channel_id=1, source_target_pairs={{3,0},{0,1},{1,2},{2,3},{7,4},{4,5},{5,6},{6,7},{11,8},{8,9},{9,10... | collective-permute-start | bytes 104 | tf_op jit(solution)/shard_map/ppermute | solution.py:12
  188.9 4.5 collective-permute-start.4
  456.7 64.4 %copy-start.1 = (f32[64,128,128]{2,1,0:T(8,128)S(1)}, f32[64,128,128]{2,1,0:T(8,128)}, u32[]{:S(2)}) copy-start(f32[64,128,128]{2,1,0:T(8,128)} %fusion.21) | copy-start | bytes 12582916
  461.0 64.5 %collective-permute-start.3 = (bf16[1,16,128]{2,1,0:T(8,128)(2,1)S(1)}, bf16[1,16,128]{2,1,0:T(8,128)(2,1)S(1)}, u32[]{:S(2)}, u32[]{:S(2)}) collective-permute-start(bf16[1,16,128]{2,1,0:T(8,128)(2,1)S(1)} %collective-permute-done.1), channel_id=1, source_target_pairs={{3,0},{0,1},{1,2},{2,3},{7,4},{4,5},{5,6},{6,7},{11,8},{8,9},{9,10... | collective-permute-start | bytes 12296 | tf_op jit(solution)/shard_map/ppermute | solution.py:12
  525.5 124.0 %copy-start.2 = (bf16[1,16,128]{2,1,0:T(8,128)(2,1)}, bf16[1,16,128]{2,1,0:T(8,128)(2,1)S(1)}, u32[]{:S(2)}) copy-start(bf16[1,16,128]{2,1,0:T(8,128)(2,1)S(1)} %collective-permute-done.3) | copy-start | bytes 12292
  650.5 3.7 copy-start.3
  650.5 31.2 %copy-start.5 = (s32[64]{0:T(128)S(1)}, s32[64]{0:T(128)}, u32[]{:S(2)}) copy-start(s32[64]{0:T(128)} %get-tuple-element.15) | copy-start | bytes 772
  650.5 31.2 %copy-start.7 = (f32[64]{0:T(128)S(1)}, f32[64]{0:T(128)}, u32[]{:S(2)}) copy-start(f32[64]{0:T(128)} %compare_convert_fusion.1) | copy-start | bytes 772
  654.2 32.0 %collective-permute-start.5 = (bf16[1,16,128]{2,1,0:T(8,128)(2,1)S(1)}, bf16[1,16,128]{2,1,0:T(8,128)(2,1)S(1)}, u32[]{:S(2)}, u32[]{:S(2)}) collective-permute-start(bf16[1,16,128]{2,1,0:T(8,128)(2,1)S(1)} %copy-done.3), channel_id=1, source_target_pairs={{3,0},{0,1},{1,2},{2,3},{7,4},{4,5},{5,6},{6,7},{11,8},{8,9},{9,10... | collective-permute-start | bytes 12296 | tf_op jit(solution)/shard_map/ppermute | solution.py:12
  814.0 3.4 copy-start.4
  814.0 3.4 copy-start.6
Sparse Core Ops, SparseCore 0:
  824.5 259.6 all-reduce.6
where the time goes:
time: 1120 us
  blocking collectives  634 us (57%)
  waiting for transfers between devices  261 us (23%)
  starting transfers between devices  125 us (11%)
  matrix products  36.7 us (3%)
  other arithmetic  29.9 us (3%)
  local copies, waits for them, and re-layouts  16.8 us (2%)
  between operations  15.2 us (1%)
    all_gather x4, blocking collectives, body(): lax.all_gather(piece_pair[0], 'rows', axis=1, tiled=True)  507 us
    psum x1, waiting for transfers between devices, body(): gram_total = lax.psum(gram_local, ('rows', 'blk'))  260 us
    unnamed x1, blocking collectives  127 us
    ppermute x6, starting transfers between devices, passed_along(): return lax.ppermute(block, axis, route)  125 us
  transfers between devices with their start and end apart: 7, of which 3 were waited for; matrix products, arithmetic and copies ran while one was open for 3% of the time, Pallas kernels for 0%

commit v1 on v0

--- a/solution.py
+++ b/solution.py
@@ -90,7 +90,8 @@
     gram_local = jnp.dot(
         flat_rows.T, flat_rows, precision=lax.Precision.HIGHEST, preferred_element_type=jnp.float32
     )
-    gram_total = lax.psum(gram_local, ("rows", "blk"))
+    shards = lax.all_gather(gram_local, ("rows", "blk"))
+    gram_total = jnp.sum(shards, axis=0)
     lower_factor = jnp.linalg.cholesky(gram_total)
     total_rows = flat_rows.shape[0] * lax.axis_size("rows") * loop_size
     root = jnp.sqrt(jnp.float32(total_rows))

time: 1120 us -> 1320 us (1.18)
  waiting for transfers between devices: 261 us -> 448 us
    all_gather x0 -> x1, waiting for transfers between devices: none -> 446 us  [body(): shards = lax.all_gather(gram_local, ('rows', 'blk'))]
    psum x1 -> x0, waiting for transfers between devices: 260 us -> none  [body(): gram_total = lax.psum(gram_local, ('rows', 'blk'))]
  transfers between devices with their start and end apart: 7 -> 7, of which waited for: 3 -> 3; matrix products, arithmetic and copies ran while one was open for 3% -> 2% of each run, Pallas kernels for 0% -> 0%
where the time goes in v1:
time: 1320 us; the launch traced here: 1310 us
  blocking collectives  634 us (48%)
  waiting for transfers between devices  448 us (34%)
  starting transfers between devices  125 us (9%)
  matrix products  36.8 us (3%)
  other arithmetic  36 us (3%)
  local copies, waits for them, and re-layouts  15.8 us (1%)
  between operations  15.3 us (1%)
    all_gather x4, blocking collectives, body(): lax.all_gather(piece_pair[0], 'rows', axis=1, tiled=True)  507 us
    all_gather x1, waiting for transfers between devices, body(): shards = lax.all_gather(gram_local, ('rows', 'blk'))  446 us
    unnamed x1, blocking collectives  127 us
    ppermute x6, starting transfers between devices, passed_along(): return lax.ppermute(block, axis, route)  125 us
  transfers between devices with their start and end apart: 7, of which 3 were waited for; matrix products, arithmetic and copies ran while one was open for 2% of the time, Pallas kernels for 0%

profile of v1, /device:TPU:1, one launch (start us, length us, event | category | flops | bytes accessed | tf_op | source)
XLA Modules:
  0.0 1310.8 jit_solution(8372121605929073758)
XLA Ops:
  7.9 4.3 collective-permute-start
  12.2 132.2 %all_gather.31 = bf16[1,1024,128]{2,1,0:T(8,128)(2,1)S(1)} all-gather(bf16[1,16,128]{2,1,0:T(8,128)(2,1)} %param.15), channel_id=1, replica_groups=mesh['rows'=64,'blk'=4] {'rows'}, dimensions={1}, use_global_device_ids=true | all-gather | bytes 266240 | tf_op jit(solution)/shard_map/all_gather | solution.py:69
  158.7 29.4 %collective-permute-start.2 = (bf16[1,16]{1,0:T(2,128)(2,1)S(1)}, bf16[1,16]{1,0:T(2,128)(2,1)S(1)}, u32[]{:S(2)}, u32[]{:S(2)}) collective-permute-start(bf16[1,16]{1,0:T(2,128)(2,1)S(1)} %collective-permute-done), channel_id=1, source_target_pairs={{3,0},{0,1},{1,2},{2,3},{7,4},{4,5},{5,6},{6,7},{11,8},{8,9},{9,10... | collective-permute-start | bytes 104 | tf_op jit(solution)/shard_map/ppermute | solution.py:12
  189.0 3.8 collective-permute-start.4
  193.7 127.1 %all-reduce.4 = (bf16[1024]{0:T(1024)(128)(2,1)S(1)}, bf16[1024]{0:T(1024)(128)(2,1)S(1)}, bf16[1024]{0:T(1024)(128)(2,1)S(1)}, bf16[1024]{0:T(1024)(128)(2,1)S(1)}) all-reduce(bf16[1024]{0:T(1024)(128)(2,1)S(1)} %dynamic-update-slice.4, bf16[1024]{0:T(1024)(128)(2,1)S(1)} %dynamic-update-slice.3, ...), channel_id=1, replica_groups=mesh['rows'=64,'blk'=4] {'rows'}, use_global_device_ids=true, to_apply=%add.1 | all-reduce | flops 4096 | bytes 16384
  321.4 4.1 fusion.21
  327.3 124.9 %all_gather.33 = bf16[1,1024,128]{2,1,0:T(8,128)(2,1)S(1)} all-gather(bf16[1,16,128]{2,1,0:T(8,128)(2,1)S(1)} %collective-permute-done.1), channel_id=1, replica_groups=mesh['rows'=64,'blk'=4] {'rows'}, dimensions={1}, use_global_device_ids=true | all-gather | bytes 266240 | tf_op jit(solution)/shard_map/all_gather | solution.py:69
  453.1 3.6 fusion.23
  456.8 4.4 fusion.16
  461.1 60.1 %collective-permute-start.3 = (bf16[1,16,128]{2,1,0:T(8,128)(2,1)S(1)}, bf16[1,16,128]{2,1,0:T(8,128)(2,1)S(1)}, u32[]{:S(2)}, u32[]{:S(2)}) collective-permute-start(bf16[1,16,128]{2,1,0:T(8,128)(2,1)S(1)} %collective-permute-done.1), channel_id=1, source_target_pairs={{3,0},{0,1},{1,2},{2,3},{7,4},{4,5},{5,6},{6,7},{11,8},{8,9},{9,10... | collective-permute-start | bytes 12296 | tf_op jit(solution)/shard_map/ppermute | solution.py:12
  521.2 4.4 fusion.49
  525.6 124.0 %all_gather.35 = bf16[1,1024,128]{2,1,0:T(8,128)(2,1)S(1)} all-gather(bf16[1,16,128]{2,1,0:T(8,128)(2,1)S(1)} %collective-permute-done.3), channel_id=1, replica_groups=mesh['rows'=64,'blk'=4] {'rows'}, dimensions={1}, use_global_device_ids=true | all-gather | bytes 266240 | tf_op jit(solution)/shard_map/all_gather | solution.py:69
  650.6 3.6 fusion.25
  654.3 27.5 %collective-permute-start.5 = (bf16[1,16,128]{2,1,0:T(8,128)(2,1)S(1)}, bf16[1,16,128]{2,1,0:T(8,128)(2,1)S(1)}, u32[]{:S(2)}, u32[]{:S(2)}) collective-permute-start(bf16[1,16,128]{2,1,0:T(8,128)(2,1)S(1)} %copy-done.3), channel_id=1, source_target_pairs={{3,0},{0,1},{1,2},{2,3},{7,4},{4,5},{5,6},{6,7},{11,8},{8,9},{9,10... | collective-permute-start | bytes 12296 | tf_op jit(solution)/shard_map/ppermute | solution.py:12
  681.8 4.4 fusion.52
  686.3 125.7 %all_gather.37 = bf16[1,1024,128]{2,1,0:T(8,128)(2,1)S(1)} all-gather(bf16[1,16,128]{2,1,0:T(8,128)(2,1)S(1)} %collective-permute-done.5), channel_id=1, replica_groups=mesh['rows'=64,'blk'=4] {'rows'}, dimensions={1}, use_global_device_ids=true | all-gather | bytes 266240 | tf_op jit(solution)/shard_map/all_gather | solution.py:69
  812.0 2.1 gather_fusion.11
  814.1 3.4 fusion.27
  817.5 4.4 fusion.55
  821.9 2.5 convolution_bitcast_fusion
  824.8 446.4 %all-gather.3.cloned.1.call-done = f32[32768,128]{1,0:T(8,128)} async-done(((f32[128,128]{1,0:T(8,128)}), f32[32768,128]{1,0:T(8,128)}) %all-gather.3.cloned.1.call-update) | async-done | bytes 16777232 | tf_op jit(solution)/shard_map/all_gather | solution.py:93
  1271.2 6.6 reduce_sum.9
  1277.9 11.7 cholesky.16
  1291.7 10.0 custom-call.6
  (78 shorter events, 24.9 us)
Async XLA Ops:
  7.2 145.4 %copy-start = (f32[1,1,2048]{2,1,0:T(1,128)S(1)}, f32[1,1,2048]{2,1,0:T(1,128)}, u32[]{:S(2)}) copy-start(f32[1,1,2048]{2,1,0:T(1,128)} %param.13) | copy-start | bytes 24580
  7.2 1264.0 %all-gather.3.cloned.1.call-start = ((), (), s32[]{:S(2)}) async-start(), calls=%async_computation | async-start | bytes 16842752 | tf_op jit(solution)/shard_map/all_gather | solution.py:93
  7.9 150.5 %collective-permute-start = (bf16[1,16]{1,0:T(2,128)(2,1)S(1)}, bf16[1,16]{1,0:T(2,128)(2,1)S(1)}, u32[]{:S(2)}, u32[]{:S(2)}) collective-permute-start(bf16[1,16]{1,0:T(2,128)(2,1)S(1)} %get-tuple-element.35), channel_id=1, source_target_pairs={{3,0},{0,1},{1,2},{2,3},{7,4},{4,5},{5,6},{6,7},{11,8},{8,9},{9,10... | collective-permute-start | bytes 104 | tf_op jit(solution)/shard_map/ppermute | solution.py:12
  12.2 315.1 %collective-permute-start.1 = (bf16[1,16,128]{2,1,0:T(8,128)(2,1)}, bf16[1,16,128]{2,1,0:T(8,128)(2,1)S(1)}, u32[]{:S(2)}, u32[]{:S(2)}) collective-permute-start(bf16[1,16,128]{2,1,0:T(8,128)(2,1)} %param.15), channel_id=1, source_target_pairs={{3,0},{0,1},{1,2},{2,3},{7,4},{4,5},{5,6},{6,7},{11,8},{8,9},{9,10... | collective-permute-start | bytes 12296 | tf_op jit(solution)/shard_map/ppermute | solution.py:12
  158.7 30.1 %collective-permute-start.2 = (bf16[1,16]{1,0:T(2,128)(2,1)S(1)}, bf16[1,16]{1,0:T(2,128)(2,1)S(1)}, u32[]{:S(2)}, u32[]{:S(2)}) collective-permute-start(bf16[1,16]{1,0:T(2,128)(2,1)S(1)} %collective-permute-done), channel_id=1, source_target_pairs={{3,0},{0,1},{1,2},{2,3},{7,4},{4,5},{5,6},{6,7},{11,8},{8,9},{9,10... | collective-permute-start | bytes 104 | tf_op jit(solution)/shard_map/ppermute | solution.py:12
  189.0 4.5 collective-permute-start.4
  456.8 64.4 %copy-start.1 = (f32[64,128,128]{2,1,0:T(8,128)S(1)}, f32[64,128,128]{2,1,0:T(8,128)}, u32[]{:S(2)}) copy-start(f32[64,128,128]{2,1,0:T(8,128)} %fusion.21) | copy-start | bytes 12582916
  461.1 64.5 %collective-permute-start.3 = (bf16[1,16,128]{2,1,0:T(8,128)(2,1)S(1)}, bf16[1,16,128]{2,1,0:T(8,128)(2,1)S(1)}, u32[]{:S(2)}, u32[]{:S(2)}) collective-permute-start(bf16[1,16,128]{2,1,0:T(8,128)(2,1)S(1)} %collective-permute-done.1), channel_id=1, source_target_pairs={{3,0},{0,1},{1,2},{2,3},{7,4},{4,5},{5,6},{6,7},{11,8},{8,9},{9,10... | collective-permute-start | bytes 12296 | tf_op jit(solution)/shard_map/ppermute | solution.py:12
  525.6 124.1 %copy-start.2 = (bf16[1,16,128]{2,1,0:T(8,128)(2,1)}, bf16[1,16,128]{2,1,0:T(8,128)(2,1)S(1)}, u32[]{:S(2)}) copy-start(bf16[1,16,128]{2,1,0:T(8,128)(2,1)S(1)} %collective-permute-done.3) | copy-start | bytes 12292
  650.6 3.7 copy-start.3
  650.6 31.2 %copy-start.5 = (s32[64]{0:T(128)S(1)}, s32[64]{0:T(128)}, u32[]{:S(2)}) copy-start(s32[64]{0:T(128)} %get-tuple-element.17) | copy-start | bytes 772
  650.6 31.2 %copy-start.7 = (f32[64]{0:T(128)S(1)}, f32[64]{0:T(128)}, u32[]{:S(2)}) copy-start(f32[64]{0:T(128)} %compare_convert_fusion.1) | copy-start | bytes 772
  654.3 32.0 %collective-permute-start.5 = (bf16[1,16,128]{2,1,0:T(8,128)(2,1)S(1)}, bf16[1,16,128]{2,1,0:T(8,128)(2,1)S(1)}, u32[]{:S(2)}, u32[]{:S(2)}) collective-permute-start(bf16[1,16,128]{2,1,0:T(8,128)(2,1)S(1)} %copy-done.3), channel_id=1, source_target_pairs={{3,0},{0,1},{1,2},{2,3},{7,4},{4,5},{5,6},{6,7},{11,8},{8,9},{9,10... | collective-permute-start | bytes 12296 | tf_op jit(solution)/shard_map/ppermute | solution.py:12
  814.1 3.4 copy-start.4
  814.1 3.4 copy-start.6
Sparse Core Ops, SparseCore 0:
  824.6 446.5 all-gather.2
